TPU v7x, 32 devices: a whole 2x2x4 slice. The times are simulated.
32 devices in a mesh: dp: 8 (over z, y), seq: 4 (over x, core).
Axes of the slice: x: 2, y: 2, z: 4, core: 2. Of those that a mesh axis runs over, the one named last changes fastest.
Arguments:
- tokens: bfloat16 [8192, 768], P(('dp', 'seq')), may hold values from -6 to 6
- ln1_gain: bfloat16 [768], P('dp'), may hold values from 0.25 to 1.75
- w_qkv: bfloat16 [768, 2304], P('dp'), may hold values from -0.21875 to 0.21875
- w_out: bfloat16 [768, 768], P('dp'), may hold values from -1.75 to 1.75
- w_ada: bfloat16 [768, 2304], P('dp'), may hold values from -0.21875 to 0.21875
- w_up: bfloat16 [768, 3072], P('dp'), may hold values from -0.21875 to 0.21875
- w_down: bfloat16 [3072, 768], P('dp'), may hold values from -0.109375 to 0.109375
- out_grad: bfloat16 [8192, 768], P(('dp', 'seq')), may hold values from -6 to 6
- layout: int32 [8, 2], P('dp'), may hold values from 256 to 896, as said below
- timestep: int32 [8], P('dp'), may hold values from 0 to 999
Outputs:
- layer_out: bfloat16 [8192, 768], P(('dp', 'seq'))
- input_grad: bfloat16 [8192, 768], P(('dp', 'seq'))
- gain_grad: float32 [768], P('dp')
- qkv_weight_grad: float32 [768, 2304], P('dp')
- out_weight_grad: float32 [768, 768], P('dp')
- ada_weight_grad: float32 [768, 2304], P('dp')
- up_weight_grad: float32 [768, 3072], P('dp')
- down_weight_grad: float32 [3072, 768], P('dp')
Inputs may be any that keep to these rules, and one draw needn't show every extreme that they name: layout[g] = (P, C): tokens below P are the prompt, the first continuation runs from P to C - 1, the second from C to 1023; P lies between 256 and 512, and each continuation holds at least a quarter of the tokens after the prompt.
All inputs are finite; a program needn't handle non-finite values.
Results may differ from a plain program's by a relative error of at most 0.017.
Values may be sent and summed in bfloat16 or wider, within the bound.
No kernel may reach another device: no remote copies, remote signals or barrier semaphores. Data moves between devices by JAX's collectives and lax.ppermute only.
A program may use at most 128 MiB of HBM per device.

v0:
```python
import math
import jax
import jax.numpy as jnp
from jax import lax
from jax.sharding import PartitionSpec as P

HEADS = 12
HEAD_DIM = 64
eps = 1e-05
neg_fill = -1e30


def layer_norm(values_in):
    average = jnp.mean(values_in, axis=-1, keepdims=True)
    centred = values_in - average
    variance = jnp.mean(centred * centred, axis=-1, keepdims=True)
    scaling = lax.rsqrt(variance + eps)
    return (centred * scaling, scaling)


def norm_back(grad_normed, normed, scaling):
    first_mean = jnp.mean(grad_normed, axis=-1, keepdims=True)
    second_mean = jnp.mean(grad_normed * normed, axis=-1, keepdims=True)
    return scaling * (grad_normed - first_mean - normed * second_mean)


def rope_tables(positions):
    half_dim = HEAD_DIM // 2
    frequency = jnp.exp(
        -math.log(10000.0) * 2.0 * jnp.arange(half_dim, dtype=jnp.float32) / HEAD_DIM
    )
    angles = positions.astype(jnp.float32)[:, None] * frequency[None, :]
    return (jnp.cos(angles), jnp.sin(angles))


def rotate(values_in, cos_table, sine_table, direction):
    half_dim = HEAD_DIM // 2
    front_half = values_in[..., :half_dim]
    back_half = values_in[..., half_dim:]
    cos_part = cos_table[:, None, :]
    sine_part = sine_table[:, None, :] * direction
    return jnp.concatenate(
        [
            front_half * cos_part - back_half * sine_part,
            back_half * cos_part + front_half * sine_part,
        ],
        axis=-1,
    )


def visible(query_pos, key_pos, prompt_end, second_start):
    query_segment = (query_pos >= prompt_end).astype(jnp.int32) + (
        query_pos >= second_start
    ).astype(jnp.int32)
    key_segment = (key_pos >= prompt_end).astype(jnp.int32) + (key_pos >= second_start).astype(
        jnp.int32
    )
    return (key_pos[None, :] < prompt_end) | (query_segment[:, None] == key_segment[None, :])


def time_table(time_steps, model_width):
    half_dim = model_width // 2
    frequency = jnp.exp(-math.log(10000.0) * jnp.arange(half_dim, dtype=jnp.float32) / half_dim)
    angles = time_steps[:, None] * frequency[None, :]
    return jnp.concatenate([jnp.cos(angles), jnp.sin(angles)], axis=1)


def left_product(left, right):
    return lax.dot_general(
        left, right, (((0,), (0,)), ((), ())), preferred_element_type=jnp.float32
    )


def right_product(left, right):
    return lax.dot_general(
        left, right, (((1,), (1,)), ((), ())), preferred_element_type=jnp.float32
    )


def split_rows(grad_full, data_count):
    return grad_full.reshape(data_count, grad_full.shape[0] // data_count, -1)


def body(tokens, ln1_gain, w_qkv, w_out, w_ada, w_up, w_down, out_grad, layout, timestep):
    seq_count = lax.axis_size("seq")
    seq_rank = lax.axis_index("seq")
    tok_rows = tokens.shape[0]
    model_width = tokens.shape[1]
    group_rows = tok_rows * seq_count
    heads_local = HEADS // seq_count
    local_width = heads_local * HEAD_DIM
    block_rows = min(512, group_rows)
    blocks = group_rows // block_rows
    gain_full, qkv_weight, out_weight = (
        lax.all_gather(ln1_gain, "dp", axis=0, tiled=True),
        lax.all_gather(w_qkv, "dp", axis=0, tiled=True),
        lax.all_gather(w_out, "dp", axis=0, tiled=True),
    )
    ada_weight, up_weight, down_weight = (
        lax.all_gather(w_ada, "dp", axis=0, tiled=True),
        lax.all_gather(w_up, "dp", axis=0, tiled=True),
        lax.all_gather(w_down, "dp", axis=0, tiled=True),
    )
    gain_float = gain_full.astype(jnp.float32)
    inputs = tokens.astype(jnp.float32)
    normed_one, scaling_one = layer_norm(inputs)
    hidden_one = (normed_one * gain_float).astype(jnp.bfloat16)
    projected = jnp.dot(hidden_one, qkv_weight, preferred_element_type=jnp.float32).reshape(
        tok_rows, 3, HEADS, HEAD_DIM
    )
    positions = seq_rank * tok_rows + jnp.arange(tok_rows, dtype=jnp.int32)
    cos_table, sine_table = rope_tables(positions)
    rotated = jnp.stack(
        [
            rotate(projected[:, 0], cos_table, sine_table, 1.0),
            rotate(projected[:, 1], cos_table, sine_table, 1.0),
            projected[:, 2],
        ],
        axis=1,
    )
    outgoing = rotated.astype(jnp.bfloat16).reshape(tok_rows, 3, seq_count, local_width)
    incoming = lax.all_to_all(outgoing, "seq", split_axis=2, concat_axis=0, tiled=True).reshape(
        group_rows, 3, heads_local, HEAD_DIM
    )
    queries = incoming[:, 0]
    keys_all = incoming[:, 1]
    values_all = incoming[:, 2]
    prompt_end = layout[0, 0]
    second_start = layout[0, 1]
    key_pos = jnp.arange(group_rows, dtype=jnp.int32)

    def scores_of(query_block, start):
        raw_scores = (
            jnp.einsum("qhd,khd->hqk", query_block, keys_all, preferred_element_type=jnp.float32)
            * 0.125
        )
        query_pos = start + jnp.arange(block_rows, dtype=jnp.int32)
        allowed = visible(query_pos, key_pos, prompt_end, second_start)
        return jnp.where(allowed[None], raw_scores, neg_fill)

    query_blocks = queries.reshape(blocks, block_rows, heads_local, HEAD_DIM)
    starts = jnp.arange(blocks, dtype=jnp.int32) * block_rows

    def forward_block(operands):
        query_block, start = operands
        scores = scores_of(query_block, start)
        row_max = jnp.max(scores, axis=-1, keepdims=True)
        exponent = jnp.exp(scores - row_max)
        row_sum = jnp.sum(exponent, axis=-1, keepdims=True)
        attn_probs = (exponent / row_sum).astype(jnp.bfloat16)
        block_out = jnp.einsum(
            "hqk,khd->qhd", attn_probs, values_all, preferred_element_type=jnp.float32
        )
        return (block_out.astype(jnp.bfloat16), (row_max + jnp.log(row_sum))[..., 0])

    attended_heads, log_sums = lax.map(forward_block, (query_blocks, starts))
    attended = lax.all_to_all(
        attended_heads.reshape(group_rows, local_width),
        "seq",
        split_axis=0,
        concat_axis=1,
        tiled=True,
    )
    middle = inputs + jnp.dot(attended, out_weight, preferred_element_type=jnp.float32)
    time_embed = time_table(timestep.astype(jnp.float32), model_width).astype(jnp.bfloat16)
    modulation = jnp.dot(time_embed, ada_weight, preferred_element_type=jnp.float32)[0]
    mod_scale = modulation[:model_width]
    mod_shift = modulation[model_width : 2 * model_width]
    mod_gate = modulation[2 * model_width :]
    normed_two, scaling_two = layer_norm(middle)
    hidden_two = (normed_two * (1.0 + mod_scale) + mod_shift).astype(jnp.bfloat16)
    pre_act = jnp.dot(hidden_two, up_weight, preferred_element_type=jnp.float32)
    gelu_vals, gelu_pull = jax.vjp(lambda inner: jax.nn.gelu(inner, approximate=True), pre_act)
    activated = gelu_vals.astype(jnp.bfloat16)
    mlp_out = jnp.dot(activated, down_weight, preferred_element_type=jnp.float32)
    result = middle + mod_gate * mlp_out
    grad_out = out_grad.astype(jnp.float32)
    grad_mlp = (mod_gate * grad_out).astype(jnp.bfloat16)
    grad_gate = jnp.sum(grad_out * mlp_out, axis=0)
    grad_wdown = left_product(activated, grad_mlp)
    grad_act = right_product(grad_mlp, down_weight)
    grad_pre = gelu_pull(grad_act)[0].astype(jnp.bfloat16)
    grad_wup = left_product(hidden_two, grad_pre)
    grad_hidden_two = right_product(grad_pre, up_weight)
    grad_scale = jnp.sum(grad_hidden_two * normed_two, axis=0)
    grad_shift = jnp.sum(grad_hidden_two, axis=0)
    grad_middle = grad_out + norm_back(grad_hidden_two * (1.0 + mod_scale), normed_two, scaling_two)
    grad_mod = jnp.concatenate([grad_scale, grad_shift, grad_gate])
    grad_branch = grad_middle.astype(jnp.bfloat16)
    grad_wout = left_product(attended, grad_branch)
    grad_attn = right_product(grad_branch, out_weight).astype(jnp.bfloat16)
    grad_heads = lax.all_to_all(grad_attn, "seq", split_axis=1, concat_axis=0, tiled=True).reshape(
        blocks, block_rows, heads_local, HEAD_DIM
    )

    def backward_block(carry, operands):
        key_grad, value_grad = carry
        query_block, start, grad_block, lse_block = operands
        scores = scores_of(query_block, start)
        attn_probs = jnp.exp(scores - lse_block[..., None])
        value_grad = value_grad + jnp.einsum(
            "hqk,qhd->khd",
            attn_probs.astype(jnp.bfloat16),
            grad_block,
            preferred_element_type=jnp.float32,
        )
        prob_grad = jnp.einsum(
            "qhd,khd->hqk", grad_block, values_all, preferred_element_type=jnp.float32
        )
        row_centre = jnp.sum(attn_probs * prob_grad, axis=-1, keepdims=True)
        score_grad = (attn_probs * (prob_grad - row_centre)).astype(jnp.bfloat16)
        query_grad = (
            jnp.einsum("hqk,khd->qhd", score_grad, keys_all, preferred_element_type=jnp.float32)
            * 0.125
        )
        key_grad = (
            key_grad
            + jnp.einsum(
                "hqk,qhd->khd", score_grad, query_block, preferred_element_type=jnp.float32
            )
            * 0.125
        )
        return ((key_grad, value_grad), query_grad)

    zero_grad = jnp.zeros((group_rows, heads_local, HEAD_DIM), jnp.float32)
    (key_grad, value_grad), query_grads = lax.scan(
        backward_block, (zero_grad, zero_grad), (query_blocks, starts, grad_heads, log_sums)
    )
    stacked = jnp.stack(
        [query_grads.reshape(group_rows, heads_local, HEAD_DIM), key_grad, value_grad], axis=1
    )
    stacked = stacked.astype(jnp.bfloat16).reshape(group_rows, 3, 1, local_width)
    returned = (
        lax.all_to_all(stacked, "seq", split_axis=0, concat_axis=2, tiled=True)
        .astype(jnp.float32)
        .reshape(tok_rows, 3, HEADS, HEAD_DIM)
    )
    grad_qkv = jnp.stack(
        [
            rotate(returned[:, 0], cos_table, sine_table, -1.0),
            rotate(returned[:, 1], cos_table, sine_table, -1.0),
            returned[:, 2],
        ],
        axis=1,
    )
    grad_qkv = grad_qkv.reshape(tok_rows, 3 * model_width).astype(jnp.bfloat16)
    grad_wqkv = left_product(hidden_one, grad_qkv)
    grad_hidden_one = right_product(grad_qkv, qkv_weight)
    grad_gain = jnp.sum(grad_hidden_one * normed_one, axis=0)
    grad_inputs = grad_middle + norm_back(grad_hidden_one * gain_float, normed_one, scaling_one)
    qkv_cols = 3 * model_width
    grad_wada = time_embed.astype(jnp.float32).reshape(-1)[:, None] * grad_mod[None, :]
    grad_joint = jnp.concatenate([grad_wqkv, grad_wada], axis=1)
    data_count = lax.axis_size("dp")
    parts = (
        lax.psum_scatter(
            split_rows(grad_gain, data_count).astype(jnp.bfloat16),
            "seq",
            scatter_dimension=1,
            tiled=True,
        ).astype(jnp.float32),
        lax.psum_scatter(
            split_rows(grad_joint, data_count).astype(jnp.bfloat16),
            "seq",
            scatter_dimension=1,
            tiled=True,
        ).astype(jnp.float32),
        lax.psum_scatter(
            split_rows(grad_wout, data_count).astype(jnp.bfloat16),
            "seq",
            scatter_dimension=1,
            tiled=True,
        ).astype(jnp.float32),
        lax.psum_scatter(
            split_rows(grad_wup, data_count).astype(jnp.bfloat16),
            "seq",
            scatter_dimension=1,
            tiled=True,
        ).astype(jnp.float32),
        lax.psum_scatter(
            split_rows(grad_wdown, data_count).astype(jnp.bfloat16),
            "seq",
            scatter_dimension=1,
            tiled=True,
        ).astype(jnp.float32),
    )
    owned = (
        lax.psum_scatter(parts[0], "dp", scatter_dimension=0, tiled=True),
        lax.psum_scatter(parts[1], "dp", scatter_dimension=0, tiled=True),
        lax.psum_scatter(parts[2], "dp", scatter_dimension=0, tiled=True),
        lax.psum_scatter(parts[3], "dp", scatter_dimension=0, tiled=True),
        lax.psum_scatter(parts[4], "dp", scatter_dimension=0, tiled=True),
    )
    spread = (
        lax.all_gather(owned[0].astype(jnp.bfloat16), "seq", axis=1, tiled=True).astype(
            jnp.float32
        ),
        lax.all_gather(owned[1].astype(jnp.bfloat16), "seq", axis=1, tiled=True).astype(
            jnp.float32
        ),
        lax.all_gather(owned[2].astype(jnp.bfloat16), "seq", axis=1, tiled=True).astype(
            jnp.float32
        ),
        lax.all_gather(owned[3].astype(jnp.bfloat16), "seq", axis=1, tiled=True).astype(
            jnp.float32
        ),
        lax.all_gather(owned[4].astype(jnp.bfloat16), "seq", axis=1, tiled=True).astype(
            jnp.float32
        ),
    )
    final_gain = spread[0].reshape(-1)
    final_joint = spread[1].reshape(spread[1].shape[1], -1)
    final_out = spread[2].reshape(spread[2].shape[1], -1)
    final_up = spread[3].reshape(spread[3].shape[1], -1)
    final_down = spread[4].reshape(spread[4].shape[1], -1)
    final_qkv = final_joint[:, :qkv_cols]
    final_ada = final_joint[:, qkv_cols:]
    return (
        result.astype(jnp.bfloat16),
        grad_inputs.astype(jnp.bfloat16),
        final_gain,
        final_qkv,
        final_out,
        final_ada,
        final_up,
        final_down,
    )


def solution(mesh):
    placed = (
        P(("dp", "seq"), None),
        P("dp"),
        P("dp", None),
        P("dp", None),
        P("dp", None),
        P("dp", None),
        P("dp", None),
        P(("dp", "seq"), None),
        P("dp", None),
        P("dp"),
    )
    return jax.shard_map(
        body,
        mesh=mesh,
        in_specs=placed,
        out_specs=(
            P(("dp", "seq"), None),
            P(("dp", "seq"), None),
            P("dp"),
            P("dp", None),
            P("dp", None),
            P("dp", None),
            P("dp", None),
            P("dp", None),
        ),
        check_vma=False,
    )
```

profile of v0, /device:TPU:0, one launch (start us, length us, event | category | flops | bytes accessed | tf_op | source)
XLA Modules:
  0.0 863.8 jit_solution(9710499089409813553)
XLA Ops:
  12.9 23.2 %all-reduce = bf16[768]{0:T(1024)(128)(2,1)S(1)} all-reduce(bf16[768]{0:T(1024)(128)(2,1)S(1)} %dynamic-update-slice), channel_id=1, replica_groups=mesh['dp'=8,'seq'=4] {'dp'}, use_global_device_ids=true, to_apply=%add | all-reduce | flops 768 | bytes 3072
  39.3 39.0 %all-gather.6.cloned.1.call-done = bf16[768,2304]{1,0:T(8,128)(2,1)} async-done(((bf16[96,2304]{1,0:T(8,128)(2,1)}), bf16[768,2304]{1,0:T(8,128)(2,1)}) %all-gather.6.cloned.1.call-update) | async-done | bytes 3538960 | tf_op jit(solution)/shard_map/all_gather | solution.py:96
  78.3 3.7 fusion.85
  83.8 3.5 all-to-all-start
  89.9 13.3 %all-to-all-done = bf16[256,3,4,192]{0,3,1,2:T(8,128)(2,1)S(1)} async-done(((bf16[256,3,4,192]{0,3,1,2:T(8,128)(2,1)}), bf16[256,3,4,192]{0,3,1,2:T(8,128)(2,1)S(1)}, u32[]{:S(2)}, u32[]{:S(2)}) %all-to-all-start) | async-done | bytes 1179680 | tf_op jit(solution)/shard_map/all_to_all | solution.py:122
  106.9 25.5 %while.30 = (s32[]{:T(128)}, bf16[2,512,3,64]{1,3,2,0:T(8,128)(2,1)S(1)}, f32[2,3,512]{2,1,0:T(4,128)}, s32[]{:T(128)}, s32[2]{0:T(128)S(1)}, /*index=5*/s32[]{:...) while((s32[]{:T(128)}, ...), condition=%wide.region_5.6_spmd.clone.clone, body=%wide.region_2.5_spmd.clone.clone.sunk | while | flops 422682112 | bytes 22220956 | solution.py:156
  108.8 1.9 convert_add_fusion.10
  111.7 2.3 fusion.141
  115.8 3.2 fusion.143
  121.5 1.9 convert_add_fusion.10
  124.5 2.3 fusion.141
  128.6 3.2 fusion.143
  133.8 3.5 all-to-all-start.1
  137.8 6.4 all-gather.10.cloned.1.call-done
  144.2 2.6 convolution_reduce_fusion
  146.8 39.1 %all-gather.8.cloned.1.call-done = bf16[768,768]{1,0:T(8,128)(2,1)} async-done(((bf16[96,768]{1,0:T(8,128)(2,1)}), bf16[768,768]{1,0:T(8,128)(2,1)}) %all-gather.8.cloned.1.call-update) | async-done | bytes 1179664 | tf_op jit(solution)/shard_map/all_gather | solution.py:97
  186.0 1.9 fusion.94
  188.1 78.6 %all-gather.12.cloned.1.call-done = bf16[768,3072]{1,0:T(8,128)(2,1)} async-done(((bf16[96,3072]{1,0:T(8,128)(2,1)}), bf16[768,3072]{1,0:T(8,128)(2,1)}) %all-gather.12.cloned.1.call-update) | async-done | bytes 4718608 | tf_op jit(solution)/shard_map/all_gather | solution.py:101
  266.7 5.5 fusion.87
  272.2 74.6 %all-gather.14.cloned.1.call-done = bf16[3072,768]{1,0:T(8,128)(2,1)} async-done(((bf16[384,768]{1,0:T(8,128)(2,1)}), bf16[3072,768]{1,0:T(8,128)(2,1)}) %all-gather.14.cloned.1.call-update) | async-done | bytes 4718608 | tf_op jit(solution)/shard_map/all_gather | solution.py:102
  346.8 6.7 fusion.56
  353.6 2.2 multiply_reduce_fusion.1
  357.4 3.5 fusion.72
  362.6 6.4 convolution_convert_fusion
  371.7 3.5 all-to-all-start.2
  375.4 3.0 convolution_convert_fusion.1
  378.4 2.6 copy.99
  381.0 5.4 all-to-all-done.2
  387.8 45.0 %while.31 = (s32[]{:T(128)}, f32[1024,3,64]{0,2,1:T(8,128)}, f32[1024,3,64]{0,2,1:T(8,128)}, bf16[2,512,3,64]{1,3,2,0:T(8,128)(2,1)}, bf16[2,512,3,64]{1,3,2,0:T...) while((s32[]{:T(128)}, f32[1024,3,64]{0,2,1:T(8,128)}, ...), condition=%wide.region_12.13_spmd.clone.clone, body=%wide.region_10.12_spmd.clone.clone.sunk | while | flops 1032363520 | bytes 110420320 | solution.py:226
  387.8 1.9 fusion.153
  392.3 1.8 convert_add_fusion.12
  395.2 3.8 multiply_reduce_fusion.7
  399.0 1.8 multiply_convert_fusion.6
  400.9 2.7 fusion.154
  404.2 4.0 fusion.155
  410.0 1.9 fusion.153
  417.5 3.8 multiply_reduce_fusion.7
  421.3 1.8 multiply_convert_fusion.6
  423.1 2.9 fusion.154
  426.6 4.3 fusion.155
  437.0 2.5 copy.80
  439.5 3.6 all-to-all-start.3
  443.4 2.2 multiply_convert_fusion.1
  445.6 30.9 %all-to-all-done.3 = bf16[1024,3,1,192]{3,1,2,0:T(4,128)(2,1)S(1)} async-done(((bf16[1024,3,1,192]{3,1,2,0:T(4,128)(2,1)}), bf16[1024,3,1,192]{3,1,2,0:T(4,128)(2,1)S(1)}, u32[]{:S(2)}, u32[]{:S(2)}) %all-to-all-start.3) | async-done | bytes 1179680 | tf_op jit(solution)/shard_map/all_to_all | solution.py:234
  476.5 2.8 copy.84
  482.6 5.5 pad_maximum_fusion
  488.0 6.7 copy.95
  497.6 1.9 copy.100
  499.5 2.1 copy_convert_fusion.1
  501.7 56.8 %reduce-scatter.27.cloned.1.call-done = bf16[24,36864]{1,0:T(8,128)(2,1)} async-done(((bf16[96,36864]{1,0:T(8,128)(2,1)}), bf16[24,36864]{1,0:T(8,128)(2,1)}) %reduce-scatter.27.cloned.1.call-update) | async-done | bytes 1769488
  558.5 2.0 copy.96
  560.5 2.5 copy_convert_fusion
  564.3 3.5 fusion.69
  567.8 5.7 all-reduce.2
  573.6 21.7 %all-reduce.3 = bf16[8,24,1]{1,0,2:T(8,128)(2,1)S(1)} all-reduce(f32[8,24,1]{1,0,2:T(8,128)S(1)} %dynamic-slice_convert_fusion), channel_id=3, replica_groups=mesh['dp'=8,'seq'=4] {'dp'}, use_global_device_ids=true, to_apply=%region_17.18.clone | all-reduce | flops 192 | bytes 1152
  596.2 5.6 all-reduce.1
  603.4 21.1 %reduce-scatter.19.cloned.1.call-done = f32[1,24,768]{2,1,0:T(8,128)} async-done(((f32[8,24,768]{2,1,0:T(8,128)}), f32[1,24,768]{2,1,0:T(8,128)}) %reduce-scatter.19.cloned.1.call-update) | async-done | bytes 73744 | tf_op jit(solution)/shard_map/reduce_scatter | solution.py:290
  625.3 5.5 all_gather.41
  631.5 59.9 %reduce-scatter.25.cloned.1.call-done = bf16[1,96,768]{2,1,0:T(8,128)(2,1)} async-done(((bf16[8,96,768]{2,1,0:T(8,128)(2,1)}), bf16[1,96,768]{2,1,0:T(8,128)(2,1)}) %reduce-scatter.25.cloned.1.call-update) | async-done | bytes 147472 | tf_op jit(solution)/shard_map/reduce_scatter | solution.py:292
  691.4 7.7 all_gather.43
  700.2 63.0 %reduce-scatter.21.cloned.1.call-done = f32[1,24,3072]{2,1,0:T(8,128)} async-done(((f32[8,24,3072]{2,1,0:T(8,128)}), f32[1,24,3072]{2,1,0:T(8,128)}) %reduce-scatter.21.cloned.1.call-update) | async-done | bytes 294928 | tf_op jit(solution)/shard_map/reduce_scatter | solution.py:291
  764.2 7.5 all_gather.42
  772.8 72.6 %reduce-scatter.17.cloned.1.call-done = f32[1,24,4608]{2,1,0:T(8,128)} async-done(((f32[8,24,4608]{2,1,0:T(8,128)}), f32[1,24,4608]{2,1,0:T(8,128)}) %reduce-scatter.17.cloned.1.call-update) | async-done | bytes 442384 | tf_op jit(solution)/shard_map/reduce_scatter | solution.py:289
  846.5 9.1 %all_gather.40 = bf16[1,96,4608]{2,1,0:T(8,128)(2,1)S(1)} all-gather(bf16[1,24,4608]{2,1,0:T(8,128)(2,1)S(1)} %convert_element_type.256), channel_id=1, replica_groups=mesh['dp'=8,'seq'=4] {'seq'}, dimensions={1}, use_global_device_ids=true | all-gather | bytes 1105920 | tf_op jit(solution)/shard_map/all_gather | solution.py:298
  (210 shorter events, 70.1 us)
Async XLA Ops:
  7.2 71.1 %all-gather.6.cloned.1.call-start = ((), (), s32[]{:S(2)}) async-start(), calls=%async_computation.12 | async-start | bytes 3981312 | tf_op jit(solution)/shard_map/all_gather | solution.py:96
  7.9 136.3 %all-gather.10.cloned.1.call-start = ((), (), s32[]{:S(2)}) async-start(), calls=%async_computation.14 | async-start | bytes 3981312 | tf_op jit(solution)/shard_map/all_gather | solution.py:100
  8.6 177.3 %all-gather.8.cloned.1.call-start = ((), (), s32[]{:S(2)}) async-start(), calls=%async_computation.13 | async-start | bytes 1327104 | tf_op jit(solution)/shard_map/all_gather | solution.py:97
  9.4 257.3 %all-gather.12.cloned.1.call-start = ((), (), s32[]{:S(2)}) async-start(), calls=%async_computation.15 | async-start | bytes 5308416 | tf_op jit(solution)/shard_map/all_gather | solution.py:101
  36.1 46.0 %copy-start.13 = (f32[768]{0:T(1024)}, f32[768]{0:T(1024)S(1)}, u32[]{:S(2)}) copy-start(f32[768]{0:T(1024)S(1)} %convert_element_type.231) | copy-start | bytes 9220
  37.2 44.8 %copy-start.16 = (f32[256]{0:T(256)}, f32[256]{0:T(256)S(1)}, u32[]{:S(2)}) copy-start(f32[256]{0:T(256)S(1)} %broadcast_multiply_fusion.6) | copy-start | bytes 3076
  38.5 43.6 %copy-start.18 = (f32[256]{0:T(256)}, f32[256]{0:T(256)S(1)}, u32[]{:S(2)}) copy-start(f32[256]{0:T(256)S(1)} %add_rsqrt_fusion.1) | copy-start | bytes 3076
  39.3 42.9 %copy-start.11 = (f32[256,32]{0,1:T(8,128)}, f32[256,32]{0,1:T(8,128)S(1)}, u32[]{:S(2)}) copy-start(f32[256,32]{0,1:T(8,128)S(1)} %get-tuple-element.453) | copy-start | bytes 98308
  82.7 6.6 copy-start.24
  83.8 19.4 %all-to-all-start = ((bf16[256,3,4,192]{0,3,1,2:T(8,128)(2,1)}), bf16[256,3,4,192]{0,3,1,2:T(8,128)(2,1)S(1)}, u32[]{:S(2)}, u32[]{:S(2)}) async-start(bf16[256,3,4,192]{0,3,1,2:T(8,128)(2,1)} %copy.70), calls=%async_computation | async-start | bytes 2359296 | tf_op jit(solution)/shard_map/all_to_all | solution.py:122
  87.4 259.4 %all-gather.14.cloned.1.call-start = ((), (), s32[]{:S(2)}) async-start(), calls=%async_computation.16 | async-start | bytes 5308416 | tf_op jit(solution)/shard_map/all_gather | solution.py:102
  132.4 14.4 %copy-start.28 = (s32[2]{0:T(128)}, s32[2]{0:T(128)S(1)}, u32[]{:S(2)}) copy-start(s32[2]{0:T(128)S(1)} %get-tuple-element.735) | copy-start | bytes 28
  132.8 53.2 %copy-start.3 = (bf16[256,768]{1,0:T(8,128)(2,1)S(1)}, bf16[256,768]{1,0:T(8,128)(2,1)}, u32[]{:S(2)}) copy-start(bf16[256,768]{1,0:T(8,128)(2,1)} %param.14) | copy-start | bytes 1179652
  133.8 52.2 %all-to-all-start.1 = ((bf16[4,256,192]{1,2,0:T(8,128)(2,1)}), bf16[4,256,192]{1,2,0:T(8,128)(2,1)S(1)}, u32[]{:S(2)}, u32[]{:S(2)}) async-start(bf16[4,256,192]{1,2,0:T(8,128)(2,1)} %copy.74), calls=%async_computation.1 | async-start | bytes 786432 | tf_op jit(solution)/shard_map/all_to_all | solution.py:157
  137.2 357.6 %reduce-scatter.29.cloned.1.call-start = ((), (), s32[]{:S(2)}) async-start(), calls=%async_computation.23 | async-start | bytes 1474560
  266.7 80.1 %copy-start.27 = (bf16[256,768]{1,0:T(8,128)(2,1)S(1)}, bf16[256,768]{1,0:T(8,128)(2,1)}, u32[]{:S(2)}) copy-start(bf16[256,768]{1,0:T(8,128)(2,1)} %param.21) | copy-start | bytes 1179652
  346.8 6.8 copy-start.25
  353.5 2.2 copy-start.8
  353.6 2.9 copy-start.26
  353.6 3.9 copy-start.30
  360.9 8.1 copy-start.5
  362.5 134.3 %reduce-scatter.23.cloned.1.call-start = ((), (), s32[]{:S(2)}) async-start(), calls=%async_computation.20 | async-start | bytes 5898240 | tf_op jit(solution)/shard_map/reduce_scatter | solution.py:280
  368.9 1.3 copy-start.7
  371.7 14.7 %all-to-all-start.2 = ((bf16[256,4,192]{0,2,1:T(8,128)(2,1)}), bf16[256,4,192]{0,2,1:T(8,128)(2,1)S(1)}, u32[]{:S(2)}, u32[]{:S(2)}) async-start(bf16[256,4,192]{0,2,1:T(8,128)(2,1)} %bitcast.16), calls=%async_computation.2 | async-start | bytes 786432 | tf_op jit(solution)/shard_map/all_to_all | solution.py:192
  375.1 122.4 %reduce-scatter.31.cloned.1.call-start = ((), (), s32[]{:S(2)}) async-start(), calls=%async_computation.24 | async-start | bytes 5898240
  381.0 6.8 copy-start.29
  389.7 9.3 %copy-start = (f32[3,512,1024]{2,1,0:T(8,128)}, f32[3,512,1024]{2,1,0:T(8,128)S(1)}, u32[]{:S(2)}) copy-start(f32[3,512,1024]{2,1,0:T(8,128)S(1)} %fusion.153) | copy-start | bytes 18874372 | tf_op jit(solution)/shard_map/while
  395.2 3.8 copy-start.2
  400.8 3.3 copy-start.1
  404.2 4.0 copy-start.9
  409.3 0.8 copy-start.10
  412.0 9.3 %copy-start = (f32[3,512,1024]{2,1,0:T(8,128)}, f32[3,512,1024]{2,1,0:T(8,128)S(1)}, u32[]{:S(2)}) copy-start(f32[3,512,1024]{2,1,0:T(8,128)S(1)} %fusion.153) | copy-start | bytes 18874372 | tf_op jit(solution)/shard_map/while
  417.5 3.8 copy-start.2
  423.1 3.5 copy-start.1
  426.6 4.3 copy-start.9
  432.0 0.8 copy-start.10
  436.9 6.4 copy-start.21
  436.9 6.4 copy-start.22
  436.9 6.4 copy-start.23
  436.9 6.5 copy-start.20
  439.5 37.0 %all-to-all-start.3 = ((bf16[1024,3,1,192]{3,1,2,0:T(4,128)(2,1)}), bf16[1024,3,1,192]{3,1,2,0:T(4,128)(2,1)S(1)}, u32[]{:S(2)}, u32[]{:S(2)}) async-start(bf16[1024,3,1,192]{3,1,2,0:T(4,128)(2,1)} %copy.80), calls=%async_computation.3 | async-start | bytes 4194304 | tf_op jit(solution)/shard_map/all_to_all | solution.py:234
  443.1 115.4 %reduce-scatter.27.cloned.1.call-start = ((), (), s32[]{:S(2)}) async-start(), calls=%async_computation.22 | async-start | bytes 8847360
  479.5 0.8 copy-start.12
  479.5 0.8 copy-start.15
  480.3 1.0 copy-start.4
  480.3 1.0 copy-start.14
  480.3 1.0 copy-start.17
  480.3 1.0 copy-start.19
  494.8 129.7 %reduce-scatter.19.cloned.1.call-start = ((), (), s32[]{:S(2)}) async-start(), calls=%async_computation.18 | async-start | bytes 663552 | tf_op jit(solution)/shard_map/reduce_scatter | solution.py:290
  496.8 194.6 %reduce-scatter.25.cloned.1.call-start = ((), (), s32[]{:S(2)}) async-start(), calls=%async_computation.21 | async-start | bytes 1327104 | tf_op jit(solution)/shard_map/reduce_scatter | solution.py:292
  497.5 265.7 %reduce-scatter.21.cloned.1.call-start = ((), (), s32[]{:S(2)}) async-start(), calls=%async_computation.19 | async-start | bytes 2654208 | tf_op jit(solution)/shard_map/reduce_scatter | solution.py:291
  501.7 343.8 %reduce-scatter.17.cloned.1.call-start = ((), (), s32[]{:S(2)}) async-start(), calls=%async_computation.17 | async-start | bytes 3981312 | tf_op jit(solution)/shard_map/reduce_scatter | solution.py:289
  564.2 38.1 %copy-start.6 = (f32[256,768]{1,0:T(8,128)S(1)}, f32[256,768]{1,0:T(8,128)}, u32[]{:S(2)}) copy-start(f32[256,768]{1,0:T(8,128)} %copy-done.5) | copy-start | bytes 2359300
Sparse Core Ops, SparseCore 0:
  10.2 68.0 all-gather.5
  80.5 63.6 all-gather.9
  146.4 39.5 all-gather.7
  188.0 78.6 all-gather.11
  268.7 78.0 all-gather.13
  362.6 27.1 reduce-scatter.28
  392.6 45.1 reduce-scatter.22
  440.3 55.2 reduce-scatter.30
  498.2 60.2 reduce-scatter.26
  562.2 62.1 reduce-scatter.18
  628.2 63.1 reduce-scatter.24
  695.2 67.9 reduce-scatter.20
  767.3 78.1 reduce-scatter.16
where the time goes:
time: 873 us; the launch traced here: 864 us
  waiting for transfers between devices  565 us (65%)
  blocking collectives  86 us (10%)
  matrix products  79.7 us (9%)
  other arithmetic  53.6 us (6%)
  local copies, waits for them, and re-layouts  46.8 us (5%)
  between operations  17.3 us (2%)
  starting transfers between devices  15.4 us (2%)
    all_gather x1, waiting for transfers between devices, body(): lax.all_gather(w_up, 'dp', axis=0, tiled=True)  78.6 us
    all_gather x1, waiting for transfers between devices, body(): lax.all_gather(w_down, 'dp', axis=0, tiled=True)  74.6 us
    reduce_scatter x1, waiting for transfers between devices, body(): lax.psum_scatter(parts[1], 'dp', scatter_dimension=0, tiled=True)  72.6 us
    reduce_scatter x1, waiting for transfers between devices, body(): lax.psum_scatter(parts[3], 'dp', scatter_dimension=0, tiled=True)  63 us
    unnamed x16, waiting for transfers between devices  60.7 us
    reduce_scatter x1, waiting for transfers between devices, body(): lax.psum_scatter(parts[4], 'dp', scatter_dimension=0, tiled=True)  59.9 us
    unnamed x4, blocking collectives  56.3 us
    all_gather x1, waiting for transfers between devices, body(): lax.all_gather(w_out, 'dp', axis=0, tiled=True)  39.1 us
  transfers between devices with their start and end apart: 17, of which 13 were waited for; matrix products, arithmetic and copies ran while one was open for 18% of the time, Pallas kernels for 0%

commit v1 on v0

--- a/solution.py
+++ b/solution.py
@@ -8,6 +8,23 @@
 HEAD_DIM = 64
 eps = 1e-05
 neg_fill = -1e30
+
+
+def joined_along(blocks, dim):
+    shape = list(blocks.shape[1:])
+    shape[dim] *= blocks.shape[0]
+    return jnp.moveaxis(blocks, 0, dim).reshape(shape)
+
+
+def collect(x, axis, dim):
+    length = lax.axis_size(axis)
+    upward = [(i, (i + 1) % length) for i in range(length)]
+    blocks = [x]
+    while len(blocks) < length:
+        blocks.append(lax.ppermute(blocks[-1], axis, upward))
+    here = lax.axis_index(axis)
+    blocks = jnp.stack(blocks)[(here - jnp.arange(length)) % length]
+    return joined_along(blocks, dim)
 
 
 def layer_norm(values_in):
@@ -98,7 +115,7 @@
     )
     ada_weight, up_weight, down_weight = (
         lax.all_gather(w_ada, "dp", axis=0, tiled=True),
-        lax.all_gather(w_up, "dp", axis=0, tiled=True),
+        collect(w_up, "dp", 0),
         lax.all_gather(w_down, "dp", axis=0, tiled=True),
     )
     gain_float = gain_full.astype(jnp.float32)

time: 873 us -> 849 us (0.973)
  waiting for transfers between devices: 565 us -> 513 us
  local copies, waits for them, and re-layouts: 46.8 us -> 59.4 us
    ppermute x0 -> x7, waiting for transfers between devices: none -> 130 us  [collect(): blocks.append(lax.ppermute(blocks[-1], axis, upward))]
    all_gather x1 -> x0, waiting for transfers between devices: 78.6 us -> none  [body(): lax.all_gather(w_up, 'dp', axis=0, tiled=True)]
    all_gather x1, waiting for transfers between devices: 39.1 us -> 0.02 us  [body(): lax.all_gather(w_out, 'dp', axis=0, tiled=True)]
    all_gather x1, waiting for transfers between devices: 39 us -> 0.01 us  [body(): lax.all_gather(w_qkv, 'dp', axis=0, tiled=True)]
    all_to_all x1, waiting for transfers between devices: 13.3 us -> 0.01 us  [body(): lax.all_to_all(outgoing, 'seq', split_axis=2, concat_axis=0, tiled=True)]
    all_gather x1, waiting for transfers between devices: 74.6 us -> 65.8 us  [body(): lax.all_gather(w_down, 'dp', axis=0, tiled=True)]
    unnamed x66 -> x69, local copies, waits for them, and re-layouts: 24 us -> 29.6 us
    unnamed x16 -> x15, waiting for transfers between devices: 60.7 us -> 59.8 us
  transfers between devices with their start and end apart: 17 -> 23, of which waited for: 13 -> 15; matrix products, arithmetic and copies ran while one was open for 18% -> 20% of each run, Pallas kernels for 0% -> 0%
where the time goes in v1:
time: 849 us; the launch traced here: 839 us
  waiting for transfers between devices  513 us (60%)
  blocking collectives  91.9 us (11%)
  matrix products  82.7 us (10%)
  local copies, waits for them, and re-layouts  59.4 us (7%)
  other arithmetic  52.9 us (6%)
  starting transfers between devices  20.9 us (2%)
  between operations  17.7 us (2%)
    ppermute x7, waiting for transfers between devices, collect(): blocks.append(lax.ppermute(blocks[-1], axis, upward))  130 us
    reduce_scatter x1, waiting for transfers between devices, body(): lax.psum_scatter(parts[1], 'dp', scatter_dimension=0, tiled=True)  72.3 us
    all_gather x1, waiting for transfers between devices, body(): lax.all_gather(w_down, 'dp', axis=0, tiled=True)  65.8 us
    reduce_scatter x1, waiting for transfers between devices, body(): lax.psum_scatter(parts[3], 'dp', scatter_dimension=0, tiled=True)  63.1 us
    unnamed x4, blocking collectives  62.1 us
    reduce_scatter x1, waiting for transfers between devices, body(): lax.psum_scatter(parts[4], 'dp', scatter_dimension=0, tiled=True)  59.8 us
    unnamed x15, waiting for transfers between devices  59.8 us
    all_to_all x1, waiting for transfers between devices, body(): lax.all_to_all(stacked, 'seq', split_axis=0, concat_axis=2, tiled=True)  30.8 us
  transfers between devices with their start and end apart: 23, of which 15 were waited for; matrix products, arithmetic and copies ran while one was open for 20% of the time, Pallas kernels for 0%

profile of v1, /device:TPU:0, one launch (start us, length us, event | category | flops | bytes accessed | tf_op | source)
XLA Modules:
  0.0 838.7 jit_solution(9161201995392866725)
XLA Ops:
  9.4 3.0 collective-permute-start
  16.8 29.0 %all-reduce = bf16[768]{0:T(1024)(128)(2,1)S(1)} all-reduce(bf16[768]{0:T(1024)(128)(2,1)S(1)} %dynamic-update-slice), channel_id=1, replica_groups=mesh['dp'=8,'seq'=4] {'dp'}, use_global_device_ids=true, to_apply=%add | all-reduce | flops 768 | bytes 3072
  50.5 1.9 bitcast_dynamic-update-slice_fusion.8
  52.4 2.3 collective-permute-start.1
  55.6 26.6 %collective-permute-done.1 = bf16[96,3072]{1,0:T(8,128)(2,1)S(1)} collective-permute-done((bf16[96,3072]{1,0:T(8,128)(2,1)S(1)}, bf16[96,3072]{1,0:T(8,128)(2,1)S(1)}, u32[]{:S(2)}, u32[]{:S(2)}) %collective-permute-start.1) | collective-permute-done | bytes 589856 | tf_op jit(solution)/shard_map/ppermute | solution.py:24
  83.3 23.1 %collective-permute-done.2 = bf16[96,3072]{1,0:T(8,128)(2,1)S(1)} collective-permute-done((bf16[96,3072]{1,0:T(8,128)(2,1)S(1)}, bf16[96,3072]{1,0:T(8,128)(2,1)S(1)}, u32[]{:S(2)}, u32[]{:S(2)}) %collective-permute-start.2) | collective-permute-done | bytes 589856 | tf_op jit(solution)/shard_map/ppermute | solution.py:24
  107.2 17.0 %collective-permute-done.3 = bf16[96,3072]{1,0:T(8,128)(2,1)S(1)} collective-permute-done((bf16[96,3072]{1,0:T(8,128)(2,1)S(1)}, bf16[96,3072]{1,0:T(8,128)(2,1)S(1)}, u32[]{:S(2)}, u32[]{:S(2)}) %collective-permute-start.3) | collective-permute-done | bytes 589856 | tf_op jit(solution)/shard_map/ppermute | solution.py:24
  125.1 21.5 %collective-permute-done.4 = bf16[96,3072]{1,0:T(8,128)(2,1)S(1)} collective-permute-done((bf16[96,3072]{1,0:T(8,128)(2,1)S(1)}, bf16[96,3072]{1,0:T(8,128)(2,1)S(1)}, u32[]{:S(2)}, u32[]{:S(2)}) %collective-permute-start.4) | collective-permute-done | bytes 589856 | tf_op jit(solution)/shard_map/ppermute | solution.py:24
  147.5 28.8 %collective-permute-done.5 = bf16[96,3072]{1,0:T(8,128)(2,1)S(1)} collective-permute-done((bf16[96,3072]{1,0:T(8,128)(2,1)S(1)}, bf16[96,3072]{1,0:T(8,128)(2,1)S(1)}, u32[]{:S(2)}, u32[]{:S(2)}) %collective-permute-start.5) | collective-permute-done | bytes 589856 | tf_op jit(solution)/shard_map/ppermute | solution.py:24
  176.4 3.6 fusion.87
  181.7 3.5 all-to-all-start
  186.2 13.4 %collective-permute-done.6 = bf16[96,3072]{1,0:T(8,128)(2,1)S(1)} collective-permute-done((bf16[96,3072]{1,0:T(8,128)(2,1)S(1)}, bf16[96,3072]{1,0:T(8,128)(2,1)S(1)}, u32[]{:S(2)}, u32[]{:S(2)}) %collective-permute-start.6) | collective-permute-done | bytes 589856 | tf_op jit(solution)/shard_map/ppermute | solution.py:24
  200.5 5.3 gather_fusion
  209.5 25.0 %while.30 = (s32[]{:T(128)}, bf16[2,512,3,64]{1,3,2,0:T(8,128)(2,1)S(1)}, f32[2,3,512]{2,1,0:T(4,128)}, s32[]{:T(128)}, s32[2]{0:T(128)S(1)}, /*index=5*/s32[]{:...) while((s32[]{:T(128)}, ...), condition=%wide.region_5.6_spmd.clone.clone, body=%wide.region_2.5_spmd.clone.clone.sunk | while | flops 422682112 | bytes 22220956 | solution.py:173
  214.1 2.3 fusion.143
  218.2 3.2 fusion.145
  226.6 2.3 fusion.143
  230.7 3.2 fusion.145
  235.9 3.5 all-to-all-start.1
  239.9 2.6 convolution_reduce_fusion
  242.6 4.2 all-to-all-done.1
  246.8 1.9 fusion.96
  249.0 5.7 fusion.89
  254.6 65.8 %all-gather.11.cloned.1.call-done = bf16[3072,768]{1,0:T(8,128)(2,1)} async-done(((bf16[384,768]{1,0:T(8,128)(2,1)}), bf16[3072,768]{1,0:T(8,128)(2,1)}) %all-gather.11.cloned.1.call-update) | async-done | bytes 4718608 | tf_op jit(solution)/shard_map/all_gather | solution.py:119
  320.4 6.6 fusion.56
  327.1 5.2 multiply_reduce_fusion.1
  332.3 3.5 fusion.72
  337.5 6.4 convolution_convert_fusion
  346.6 3.5 all-to-all-start.2
  350.3 3.0 convolution_convert_fusion.1
  353.3 2.5 copy.99
  355.8 5.5 all-to-all-done.2
  362.7 44.7 %while.31 = (s32[]{:T(128)}, f32[1024,3,64]{0,2,1:T(8,128)}, f32[1024,3,64]{0,2,1:T(8,128)}, bf16[2,512,3,64]{1,3,2,0:T(8,128)(2,1)}, bf16[2,512,3,64]{1,3,2,0:T...) while((s32[]{:T(128)}, f32[1024,3,64]{0,2,1:T(8,128)}, ...), condition=%wide.region_12.13_spmd.clone.clone, body=%wide.region_10.12_spmd.clone.clone.sunk | while | flops 1032363520 | bytes 110420320 | solution.py:243
  362.7 1.9 fusion.155
  370.0 3.8 multiply_reduce_fusion.7
  375.7 2.7 fusion.156
  379.0 4.0 fusion.157
  384.9 1.9 fusion.155
  392.2 3.8 multiply_reduce_fusion.7
  397.8 2.9 fusion.156
  401.3 4.3 fusion.157
  411.6 2.5 copy.80
  414.2 3.6 all-to-all-start.3
  418.1 2.2 multiply_convert_fusion.1
  420.3 30.8 %all-to-all-done.3 = bf16[1024,3,1,192]{3,1,2,0:T(4,128)(2,1)S(1)} async-done(((bf16[1024,3,1,192]{3,1,2,0:T(4,128)(2,1)}), bf16[1024,3,1,192]{3,1,2,0:T(4,128)(2,1)S(1)}, u32[]{:S(2)}, u32[]{:S(2)}) %all-to-all-start.3) | async-done | bytes 1179680 | tf_op jit(solution)/shard_map/all_to_all | solution.py:251
  451.1 2.8 copy.84
  457.2 5.5 pad_maximum_fusion
  462.6 6.7 copy.95
  474.0 2.1 copy_convert_fusion.1
  476.2 57.1 %reduce-scatter.27.cloned.1.call-done = bf16[24,36864]{1,0:T(8,128)(2,1)} async-done(((bf16[96,36864]{1,0:T(8,128)(2,1)}), bf16[24,36864]{1,0:T(8,128)(2,1)}) %reduce-scatter.27.cloned.1.call-update) | async-done | bytes 1769488
  533.3 2.0 copy.96
  535.3 2.4 copy_convert_fusion
  539.0 3.5 fusion.69
  542.5 5.7 all-reduce.2
  548.4 21.7 %all-reduce.3 = bf16[8,24,1]{1,0,2:T(8,128)(2,1)S(1)} all-reduce(f32[8,24,1]{1,0,2:T(8,128)S(1)} %dynamic-slice_convert_fusion), channel_id=3, replica_groups=mesh['dp'=8,'seq'=4] {'dp'}, use_global_device_ids=true, to_apply=%region_17.18.clone | all-reduce | flops 192 | bytes 1152
  571.0 5.6 all-reduce.1
  578.2 21.1 %reduce-scatter.19.cloned.1.call-done = f32[1,24,768]{2,1,0:T(8,128)} async-done(((f32[8,24,768]{2,1,0:T(8,128)}), f32[1,24,768]{2,1,0:T(8,128)}) %reduce-scatter.19.cloned.1.call-update) | async-done | bytes 73744 | tf_op jit(solution)/shard_map/reduce_scatter | solution.py:307
  600.2 5.5 all_gather.37
  606.3 59.8 %reduce-scatter.25.cloned.1.call-done = bf16[1,96,768]{2,1,0:T(8,128)(2,1)} async-done(((bf16[8,96,768]{2,1,0:T(8,128)(2,1)}), bf16[1,96,768]{2,1,0:T(8,128)(2,1)}) %reduce-scatter.25.cloned.1.call-update) | async-done | bytes 147472 | tf_op jit(solution)/shard_map/reduce_scatter | solution.py:309
  666.2 7.7 all_gather.39
  675.0 63.1 %reduce-scatter.21.cloned.1.call-done = f32[1,24,3072]{2,1,0:T(8,128)} async-done(((f32[8,24,3072]{2,1,0:T(8,128)}), f32[1,24,3072]{2,1,0:T(8,128)}) %reduce-scatter.21.cloned.1.call-update) | async-done | bytes 294928 | tf_op jit(solution)/shard_map/reduce_scatter | solution.py:308
  739.1 7.5 all_gather.38
  747.7 72.3 %reduce-scatter.17.cloned.1.call-done = f32[1,24,4608]{2,1,0:T(8,128)} async-done(((f32[8,24,4608]{2,1,0:T(8,128)}), f32[1,24,4608]{2,1,0:T(8,128)}) %reduce-scatter.17.cloned.1.call-update) | async-done | bytes 442384 | tf_op jit(solution)/shard_map/reduce_scatter | solution.py:306
  821.0 9.1 %all_gather.36 = bf16[1,96,4608]{2,1,0:T(8,128)(2,1)S(1)} all-gather(bf16[1,24,4608]{2,1,0:T(8,128)(2,1)S(1)} %convert_element_type.256), channel_id=1, replica_groups=mesh['dp'=8,'seq'=4] {'seq'}, dimensions={1}, use_global_device_ids=true | all-gather | bytes 1105920 | tf_op jit(solution)/shard_map/all_gather | solution.py:315
  (228 shorter events, 85.1 us)
Async XLA Ops:
  7.2 169.2 %all-gather.5.cloned.1.call-start = ((), (), s32[]{:S(2)}) async-start(), calls=%async_computation.12 | async-start | bytes 3981312 | tf_op jit(solution)/shard_map/all_gather | solution.py:113
  7.9 232.0 %all-gather.9.cloned.1.call-start = ((), (), s32[]{:S(2)}) async-start(), calls=%async_computation.14 | async-start | bytes 3981312 | tf_op jit(solution)/shard_map/all_gather | solution.py:117
  8.6 233.9 %all-gather.7.cloned.1.call-start = ((), (), s32[]{:S(2)}) async-start(), calls=%async_computation.13 | async-start | bytes 1327104 | tf_op jit(solution)/shard_map/all_gather | solution.py:114
  9.4 311.0 %all-gather.11.cloned.1.call-start = ((), (), s32[]{:S(2)}) async-start(), calls=%async_computation.15 | async-start | bytes 5308416 | tf_op jit(solution)/shard_map/all_gather | solution.py:119
  9.4 43.0 %collective-permute-start = (bf16[96,3072]{1,0:T(8,128)(2,1)}, bf16[96,3072]{1,0:T(8,128)(2,1)S(1)}, u32[]{:S(2)}, u32[]{:S(2)}) collective-permute-start(bf16[96,3072]{1,0:T(8,128)(2,1)} %param.19), channel_id=1, source_target_pairs={{0,4},{4,8},{8,12},{12,16},{16,20},{20,24},{24,28},{28,0},{1,5},{5... | collective-permute-start | bytes 1769480 | tf_op jit(solution)/shard_map/ppermute | solution.py:24
  45.8 130.5 %copy-start.13 = (f32[768]{0:T(1024)}, f32[768]{0:T(1024)S(1)}, u32[]{:S(2)}) copy-start(f32[768]{0:T(1024)S(1)} %convert_element_type.231) | copy-start | bytes 9220
  47.0 129.4 %copy-start.16 = (f32[256]{0:T(256)}, f32[256]{0:T(256)S(1)}, u32[]{:S(2)}) copy-start(f32[256]{0:T(256)S(1)} %broadcast_multiply_fusion.6) | copy-start | bytes 3076
  48.3 128.0 %copy-start.18 = (f32[256]{0:T(256)}, f32[256]{0:T(256)S(1)}, u32[]{:S(2)}) copy-start(f32[256]{0:T(256)S(1)} %add_rsqrt_fusion.1) | copy-start | bytes 3076
  50.5 129.7 %copy-start.11 = (f32[256,32]{0,1:T(8,128)}, f32[256,32]{0,1:T(8,128)S(1)}, u32[]{:S(2)}) copy-start(f32[256,32]{0,1:T(8,128)S(1)} %get-tuple-element.453) | copy-start | bytes 98308
  52.4 123.9 %copy-start.3 = (bf16[256,768]{1,0:T(8,128)(2,1)S(1)}, bf16[256,768]{1,0:T(8,128)(2,1)}, u32[]{:S(2)}) copy-start(bf16[256,768]{1,0:T(8,128)(2,1)} %param.14) | copy-start | bytes 1179652
  52.4 29.7 %collective-permute-start.1 = (bf16[96,3072]{1,0:T(8,128)(2,1)S(1)}, bf16[96,3072]{1,0:T(8,128)(2,1)S(1)}, u32[]{:S(2)}, u32[]{:S(2)}) collective-permute-start(bf16[96,3072]{1,0:T(8,128)(2,1)S(1)} %collective-permute-done), channel_id=1, source_target_pairs={{0,4},{4,8},{8,12},{12,16},{16,20},{20,24},{24,28},{28,0},{1,5},{5... | collective-permute-start | bytes 1769480 | tf_op jit(solution)/shard_map/ppermute | solution.py:24
  82.2 24.2 %collective-permute-start.2 = (bf16[96,3072]{1,0:T(8,128)(2,1)S(1)}, bf16[96,3072]{1,0:T(8,128)(2,1)S(1)}, u32[]{:S(2)}, u32[]{:S(2)}) collective-permute-start(bf16[96,3072]{1,0:T(8,128)(2,1)S(1)} %collective-permute-done.1), channel_id=1, source_target_pairs={{0,4},{4,8},{8,12},{12,16},{16,20},{20,24},{24,28},{28,0},{1,5},{5... | collective-permute-start | bytes 1769480 | tf_op jit(solution)/shard_map/ppermute | solution.py:24
  106.4 17.8 %collective-permute-start.3 = (bf16[96,3072]{1,0:T(8,128)(2,1)S(1)}, bf16[96,3072]{1,0:T(8,128)(2,1)S(1)}, u32[]{:S(2)}, u32[]{:S(2)}) collective-permute-start(bf16[96,3072]{1,0:T(8,128)(2,1)S(1)} %collective-permute-done.2), channel_id=1, source_target_pairs={{0,4},{4,8},{8,12},{12,16},{16,20},{20,24},{24,28},{28,0},{1,5},{5... | collective-permute-start | bytes 1769480 | tf_op jit(solution)/shard_map/ppermute | solution.py:24
  124.2 22.4 %collective-permute-start.4 = (bf16[96,3072]{1,0:T(8,128)(2,1)S(1)}, bf16[96,3072]{1,0:T(8,128)(2,1)S(1)}, u32[]{:S(2)}, u32[]{:S(2)}) collective-permute-start(bf16[96,3072]{1,0:T(8,128)(2,1)S(1)} %collective-permute-done.3), channel_id=1, source_target_pairs={{0,4},{4,8},{8,12},{12,16},{16,20},{20,24},{24,28},{28,0},{1,5},{5... | collective-permute-start | bytes 1769480 | tf_op jit(solution)/shard_map/ppermute | solution.py:24
  146.6 29.7 %collective-permute-start.5 = (bf16[96,3072]{1,0:T(8,128)(2,1)S(1)}, bf16[96,3072]{1,0:T(8,128)(2,1)S(1)}, u32[]{:S(2)}, u32[]{:S(2)}) collective-permute-start(bf16[96,3072]{1,0:T(8,128)(2,1)S(1)} %collective-permute-done.4), channel_id=1, source_target_pairs={{0,4},{4,8},{8,12},{12,16},{16,20},{20,24},{24,28},{28,0},{1,5},{5... | collective-permute-start | bytes 1769480 | tf_op jit(solution)/shard_map/ppermute | solution.py:24
  176.3 23.3 %collective-permute-start.6 = (bf16[96,3072]{1,0:T(8,128)(2,1)S(1)}, bf16[96,3072]{1,0:T(8,128)(2,1)S(1)}, u32[]{:S(2)}, u32[]{:S(2)}) collective-permute-start(bf16[96,3072]{1,0:T(8,128)(2,1)S(1)} %collective-permute-done.5), channel_id=1, source_target_pairs={{0,4},{4,8},{8,12},{12,16},{16,20},{20,24},{24,28},{28,0},{1,5},{5... | collective-permute-start | bytes 1769480 | tf_op jit(solution)/shard_map/ppermute | solution.py:24
  181.7 24.1 %all-to-all-start = ((bf16[256,3,4,192]{0,3,1,2:T(8,128)(2,1)}), bf16[256,3,4,192]{0,3,1,2:T(8,128)(2,1)S(1)}, u32[]{:S(2)}, u32[]{:S(2)}) async-start(bf16[256,3,4,192]{0,3,1,2:T(8,128)(2,1)} %copy.70), calls=%async_computation | async-start | bytes 2359296 | tf_op jit(solution)/shard_map/all_to_all | solution.py:139
  234.6 5.4 copy-start.26
  235.9 10.9 %all-to-all-start.1 = ((bf16[4,256,192]{1,2,0:T(8,128)(2,1)}), bf16[4,256,192]{1,2,0:T(8,128)(2,1)S(1)}, u32[]{:S(2)}, u32[]{:S(2)}) async-start(bf16[4,256,192]{1,2,0:T(8,128)(2,1)} %copy.74), calls=%async_computation.1 | async-start | bytes 786432 | tf_op jit(solution)/shard_map/all_to_all | solution.py:174
  239.4 230.1 %reduce-scatter.29.cloned.1.call-start = ((), (), s32[]{:S(2)}) async-start(), calls=%async_computation.22 | async-start | bytes 1474560
  249.0 71.4 %copy-start.25 = (bf16[256,768]{1,0:T(8,128)(2,1)S(1)}, bf16[256,768]{1,0:T(8,128)(2,1)}, u32[]{:S(2)}) copy-start(bf16[256,768]{1,0:T(8,128)(2,1)} %param.21) | copy-start | bytes 1179652
  327.0 5.2 copy-start.8
  327.0 5.2 copy-start.24
  327.0 5.3 copy-start.28
  335.8 8.1 copy-start.5
  337.4 134.0 %reduce-scatter.23.cloned.1.call-start = ((), (), s32[]{:S(2)}) async-start(), calls=%async_computation.19 | async-start | bytes 5898240 | tf_op jit(solution)/shard_map/reduce_scatter | solution.py:297
  343.9 1.3 copy-start.7
  346.6 14.8 %all-to-all-start.2 = ((bf16[256,4,192]{0,2,1:T(8,128)(2,1)}), bf16[256,4,192]{0,2,1:T(8,128)(2,1)S(1)}, u32[]{:S(2)}, u32[]{:S(2)}) async-start(bf16[256,4,192]{0,2,1:T(8,128)(2,1)} %bitcast.26), calls=%async_computation.2 | async-start | bytes 786432 | tf_op jit(solution)/shard_map/all_to_all | solution.py:209
  350.1 122.0 %reduce-scatter.31.cloned.1.call-start = ((), (), s32[]{:S(2)}) async-start(), calls=%async_computation.23 | async-start | bytes 5898240
  355.8 6.9 copy-start.27
  364.7 9.1 %copy-start = (f32[3,512,1024]{2,1,0:T(8,128)}, f32[3,512,1024]{2,1,0:T(8,128)S(1)}, u32[]{:S(2)}) copy-start(f32[3,512,1024]{2,1,0:T(8,128)S(1)} %fusion.155) | copy-start | bytes 18874372 | tf_op jit(solution)/shard_map/while
  370.0 3.8 copy-start.2
  375.7 3.3 copy-start.1
  379.0 4.0 copy-start.9
  384.1 0.8 copy-start.10
  386.8 9.1 %copy-start = (f32[3,512,1024]{2,1,0:T(8,128)}, f32[3,512,1024]{2,1,0:T(8,128)S(1)}, u32[]{:S(2)}) copy-start(f32[3,512,1024]{2,1,0:T(8,128)S(1)} %fusion.155) | copy-start | bytes 18874372 | tf_op jit(solution)/shard_map/while
  392.2 3.8 copy-start.2
  397.8 3.5 copy-start.1
  401.3 4.3 copy-start.9
  406.6 0.8 copy-start.10
  411.6 6.4 copy-start.21
  411.6 6.4 copy-start.22
  411.6 6.4 copy-start.23
  411.6 6.5 copy-start.20
  414.2 36.9 %all-to-all-start.3 = ((bf16[1024,3,1,192]{3,1,2,0:T(4,128)(2,1)}), bf16[1024,3,1,192]{3,1,2,0:T(4,128)(2,1)S(1)}, u32[]{:S(2)}, u32[]{:S(2)}) async-start(bf16[1024,3,1,192]{3,1,2,0:T(4,128)(2,1)} %copy.80), calls=%async_computation.3 | async-start | bytes 4194304 | tf_op jit(solution)/shard_map/all_to_all | solution.py:251
  417.8 115.5 %reduce-scatter.27.cloned.1.call-start = ((), (), s32[]{:S(2)}) async-start(), calls=%async_computation.21 | async-start | bytes 8847360
  454.1 0.8 copy-start.12
  454.1 0.8 copy-start.15
  454.8 1.0 copy-start.4
  454.8 1.0 copy-start.14
  454.9 1.0 copy-start.17
  454.9 1.0 copy-start.19
  469.4 129.9 %reduce-scatter.19.cloned.1.call-start = ((), (), s32[]{:S(2)}) async-start(), calls=%async_computation.17 | async-start | bytes 663552 | tf_op jit(solution)/shard_map/reduce_scatter | solution.py:307
  471.4 194.8 %reduce-scatter.25.cloned.1.call-start = ((), (), s32[]{:S(2)}) async-start(), calls=%async_computation.20 | async-start | bytes 1327104 | tf_op jit(solution)/shard_map/reduce_scatter | solution.py:309
  472.0 266.1 %reduce-scatter.21.cloned.1.call-start = ((), (), s32[]{:S(2)}) async-start(), calls=%async_computation.18 | async-start | bytes 2654208 | tf_op jit(solution)/shard_map/reduce_scatter | solution.py:308
  476.1 343.8 %reduce-scatter.17.cloned.1.call-start = ((), (), s32[]{:S(2)}) async-start(), calls=%async_computation.16 | async-start | bytes 3981312 | tf_op jit(solution)/shard_map/reduce_scatter | solution.py:306
  539.0 38.1 %copy-start.6 = (f32[256,768]{1,0:T(8,128)S(1)}, f32[256,768]{1,0:T(8,128)}, u32[]{:S(2)}) copy-start(f32[256,768]{1,0:T(8,128)} %copy-done.5) | copy-start | bytes 2359300
Sparse Core Ops, SparseCore 0:
  10.2 84.6 all-gather.4
  97.0 97.7 all-gather.8
  197.0 42.6 all-gather.6
  241.7 78.6 all-gather.10
  337.5 27.2 reduce-scatter.28
  367.3 45.1 reduce-scatter.22
  415.0 55.1 reduce-scatter.30
  472.9 60.3 reduce-scatter.26
  537.1 62.0 reduce-scatter.18
  602.9 63.2 reduce-scatter.24
  670.1 67.9 reduce-scatter.20
  742.0 77.9 reduce-scatter.16
